TPU v7x, 32 devices: a whole 2x2x4 slice. The times are simulated.
32 devices in a mesh: rows: 8 (over y, x, core), feat: 4 (over z).
Axes of the slice: x: 2, y: 2, z: 4, core: 2. Of those that a mesh axis runs over, the one named last changes fastest.
Arguments:
- queries: bfloat16 [49152, 4096], P('rows', 'feat'), may hold values from -6 to 6
- projection: bfloat16 [4096, 128], P('feat'), may hold values from -0.09375 to 0.09375
- models: float32 [64, 128], replicated, may hold values from -0.5 to 0.5
- first: int32 [49152], P('rows'), may hold values from 0 to 63
- second: int32 [49152], P('rows'), may hold values from 0 to 63
- wins: int32 [49152], P('rows'), may hold values 0 or 1
Outputs:
- update_proj: float32 [4096, 128], P('feat')
- update_models: float32 [64, 128], replicated
- loss: float32 [], replicated
All inputs are finite; a program needn't handle non-finite values. No bound on the sum of `wins` on one device may be relied on, other than what follows from the above.
Results may differ from a plain program's by a relative error of at most 0.00045.
The roundings to bfloat16 on the way count: a program that leaves them out, or rounds other values in their place, can miss the bound.
Values may be sent and summed in bfloat16 or wider, within the bound.
A program may use at most 64 MiB of HBM per device.

v0:
```python
import jax
import jax.numpy as jnp
from jax import lax
from jax.sharding import PartitionSpec as P

D = 4096
R = 128
NM = 64


def pair_gap(models, first, second):
    return jnp.take(models, first, axis=0) - jnp.take(models, second, axis=0)


def pick_table(models, first, second):
    labels = jnp.arange(models.shape[0], dtype=jnp.int32)[:, None]
    return (labels == first[None, :]).astype(jnp.float32) - (labels == second[None, :]).astype(
        jnp.float32
    )


def body(queries, projection, models, first, second, wins):
    local_rows = queries.shape[0]
    total_rows = float(local_rows * lax.axis_size("rows"))
    partial_value = jnp.dot(queries, projection, preferred_element_type=jnp.float32)
    gap = pair_gap(models, first, second)
    margin = lax.psum(jnp.sum(partial_value * gap, axis=-1), "feat")
    sign = 2.0 * wins.astype(jnp.float32) - 1.0
    loss_part = jnp.sum(jax.nn.softplus(-sign * margin)) / total_rows
    coef = -sign * jax.nn.sigmoid(-sign * margin) / total_rows
    back = (coef[:, None] * gap).astype(jnp.bfloat16)
    pick = pick_table(models, first, second)
    model_part = jnp.dot(pick, coef[:, None] * partial_value, precision=lax.Precision.HIGHEST)
    feat_count = float(lax.axis_size("feat"))
    grad_models, loss = lax.psum((model_part, loss_part / feat_count), ("rows", "feat"))
    model_square = jnp.sum(grad_models * grad_models)
    entries = jnp.sqrt(jnp.float32(D * R + NM * R))
    grad_local = jnp.dot(queries.T, back, preferred_element_type=jnp.float32)
    grad_proj = lax.psum(grad_local, "rows")
    square = lax.psum(jnp.sum(grad_proj * grad_proj), "feat")
    scale = entries / (jnp.sqrt(square + model_square) + 1e-06)
    update_proj = scale * grad_proj
    return (update_proj, scale * grad_models, loss)


def solution(mesh):
    in_specs = (P("rows", "feat"), P("feat", None), P(), P("rows"), P("rows"), P("rows"))
    out_specs = (P("feat", None), P(), P())
    return jax.shard_map(body, mesh=mesh, in_specs=in_specs, out_specs=out_specs, check_vma=False)
```

profile of v0, /device:TPU:0, one launch (start us, length us, event | category | flops | bytes accessed | tf_op | source)
XLA Modules:
  0.0 177.5 jit_solution(17190203566094224995)
XLA Ops:
  7.2 0.0 copy-start
  7.2 0.0 copy-start.1
  7.2 0.0 all-reduce.3.cloned.1.call-start
  7.2 0.7 fusion.14
  8.0 0.8 compare_and_fusion
  8.8 0.7 fusion.13
  9.5 0.0 copy-done.1
  9.5 20.9 %gather_fusion.1 = f32[6144,128]{1,0:T(8,128)} fusion(f32[64,128]{1,0:T(8,128)S(1)} %copy-done.1, s32[6144]{0:T(1024)S(1)} %fusion.14), kind=kCustom, calls=%fused_computation.1.clone | custom fusion | bytes 6316032 | tf_op jit(solution)/shard_map/jit(_take)/gather | solution.py:12
  30.4 2.4 %copy.10 = f32[6144,128]{0,1:T(8,128)S(1)} copy(f32[6144,128]{1,0:T(8,128)} %gather_fusion.1) | data formatting | bytes 6291456 | tf_op jit(solution)/shard_map/jit(_take)/gather | solution.py:12
  32.8 20.9 %gather_fusion = f32[6144,128]{1,0:T(8,128)} fusion(f32[64,128]{1,0:T(8,128)S(1)} %copy-done.1, s32[6144]{0:T(1024)S(1)} %fusion.13), kind=kCustom, calls=%fused_computation.clone | custom fusion | bytes 6316032 | tf_op jit(solution)/shard_map/jit(_take)/gather | solution.py:12
  53.7 3.5 %copy.9 = f32[6144,128]{0,1:T(8,128)} copy(f32[6144,128]{1,0:T(8,128)} %gather_fusion) | data formatting | bytes 6291456 | tf_op jit(solution)/shard_map/jit(_take)/gather | solution.py:12
  57.2 0.0 copy-done
  57.2 0.0 copy-start.4
  57.2 11.7 %multiply_reduce_fusion = (f32[6144]{0:T(1024)S(1)}, f32[6144,128]{0,1:T(8,128)}) fusion(f32[6144,128]{0,1:T(8,128)S(1)} %copy.10, pred[6144]{0:T(1024)(128)(4,1)S(1)} %get-tuple-element.13, f32[6144,128]{0,1:T(8,128)} %copy.9, pred[6144]{0:T(1024)(128)(4,1)S(1)} %get-tuple-element.14, bf16[6144,1024]{1,0:T(8,128)(2,1)} %param.8, ...), kind=kOutput, calls=%fused_computation.6 | convolution fusion | flops 1614538752 | bytes 22319104 | tf_op jit(solution)/shard_map/dot_general | solution.py:25
  68.9 20.8 %psum.35 = f32[6144]{0:T(1024)S(1)} all-reduce(f32[6144]{0:T(1024)S(1)} %get-tuple-element.11), channel_id=1, replica_groups=mesh['rows'=8,'feat'=4] {'feat'}, use_global_device_ids=true, to_apply=%region_1.3 | all-reduce | flops 6144 | bytes 49152 | tf_op jit(solution)/shard_map/psum | solution.py:27
  89.6 0.0 copy-done.4
  89.6 0.6 fusion.11
  90.3 0.0 copy-start.2
  90.3 0.0 copy-start.3
  90.3 8.3 %fusion.8 = f32[1024,128]{0,1:T(8,128)} fusion(bf16[6144,1024]{1,0:T(8,128)(2,1)} %param.8, f32[6144]{0:T(1024)S(1)} %get-tuple-element.10, f32[6144,128]{0,1:T(8,128)S(1)} %copy.10, f32[6144,128]{0,1:T(8,128)} %copy.9, pred[6144]{0:T(1024)(128)(4,1)S(1)} %get-tuple-element.13, pred[6144]{0:T(1024)(128)(4,1)S(1)} %get-tuple-element.14), kind=kOutput, calls=%fused_computation.15 | convolution fusion | flops 1614544896 | bytes 19435520 | tf_op jit(solution)/shard_map/dot_general | solution.py:38
  98.6 0.0 all-reduce.3.cloned.1.call-update
  99.2 0.0 copy-done.2
  99.2 0.0 copy-done.3
  99.3 5.2 %fusion = f32[64,128]{1,0:T(8,128)S(1)} fusion(f32[6144,128]{0,1:T(8,128)} %get-tuple-element.12, f32[6144]{0:T(1024)S(1)} %get-tuple-element.10, s32[6144]{0:T(1024)S(1)} %copy-done.2, s32[6144]{0:T(1024)S(1)} %copy-done.3), kind=kOutput, calls=%fused_computation.3 | convolution fusion | flops 606732288 | bytes 3252224 | tf_op jit(solution)/shard_map/dot_general | solution.py:33
  104.4 38.9 %all-reduce = (f32[64,128]{1,0:T(8,128)S(1)}, f32[]{:T(128)}) all-reduce(f32[64,128]{1,0:T(8,128)S(1)} %fusion, f32[]{:T(128)S(6)} %div.20), channel_id=1, replica_groups=mesh['rows'=8,'feat'=4] {'rows','feat'}, use_global_device_ids=true, to_apply=%region_5.7 | all-reduce | flops 8193 | bytes 65544 | tf_op jit(solution)/shard_map/psum | solution.py:35
  143.3 8.6 %all-reduce.3.cloned.1.call-done = f32[1024,128]{0,1:T(8,128)} async-done(((f32[1024,128]{0,1:T(8,128)}), f32[1024,128]{0,1:T(8,128)}) %all-reduce.3.cloned.1.call-update) | async-done | bytes 524304 | tf_op jit(solution)/shard_map/psum | solution.py:39
  151.9 1.8 %multiply_reduce_fusion.1 = f32[]{:T(128)} fusion(f32[1024,128]{0,1:T(8,128)} %all-reduce.3.cloned.1.call-done), kind=kLoop, calls=%fused_computation.18 | loop fusion | flops 262143 | bytes 524292 | tf_op jit(solution)/shard_map/reduce_sum | solution.py:40
  153.7 0.6 multiply_reduce_fusion.2
  154.3 12.2 %psum.37 = f32[]{:T(128)} all-reduce(f32[]{:T(128)} %multiply_reduce_fusion.1), channel_id=1, replica_groups=mesh['rows'=8,'feat'=4] {'feat'}, use_global_device_ids=true, to_apply=%region_4.6 | all-reduce | flops 1 | bytes 8 | tf_op jit(solution)/shard_map/psum | solution.py:40
  168.0 0.6 broadcast_multiply_fusion.1
  168.6 1.1 broadcast_multiply_fusion
  169.7 1.0 copy.11
Async XLA Ops:
  7.2 50.0 %copy-start = (bf16[1024,128]{1,0:T(8,128)(2,1)S(1)}, bf16[1024,128]{1,0:T(8,128)(2,1)}, u32[]{:S(2)}) copy-start(bf16[1024,128]{1,0:T(8,128)(2,1)} %param.9) | copy-start | bytes 786436
  7.2 2.3 %copy-start.1 = (f32[64,128]{1,0:T(8,128)S(1)}, f32[64,128]{1,0:T(8,128)}, u32[]{:S(2)}) copy-start(f32[64,128]{1,0:T(8,128)} %param.10) | copy-start | bytes 98308
  7.2 144.8 %all-reduce.3.cloned.1.call-start = ((), (), s32[]{:S(2)}) async-start(), calls=%async_computation | async-start | bytes 1048576 | tf_op jit(solution)/shard_map/psum | solution.py:39
  57.2 32.4 %copy-start.4 = (s32[6144]{0:T(1024)S(1)}, s32[6144]{0:T(1024)}, u32[]{:S(2)}) copy-start(s32[6144]{0:T(1024)} %param.13) | copy-start | bytes 73732
  90.3 9.0 %copy-start.2 = (s32[6144]{0:T(1024)S(1)}, s32[6144]{0:T(1024)}, u32[]{:S(2)}) copy-start(s32[6144]{0:T(1024)} %param.12) | copy-start | bytes 73732
  90.3 9.0 %copy-start.3 = (s32[6144]{0:T(1024)S(1)}, s32[6144]{0:T(1024)}, u32[]{:S(2)}) copy-start(s32[6144]{0:T(1024)} %param.11) | copy-start | bytes 73732
Sparse Core Ops, SparseCore 0:
  98.7 53.1 all-reduce.2
where the time goes:
time: 178 us
  blocking collectives  71.9 us (40%)
  local copies, waits for them, and re-layouts  48.7 us (27%)
  matrix products  25.1 us (14%)
  between operations  16.1 us (9%)
  waiting for transfers between devices  8.62 us (5%)
  other arithmetic  6.98 us (4%)
    gather x4, local copies, waits for them, and re-layouts, pair_gap(): return jnp.take(models, first, axis=0) - jnp.take(models, second, axis=0)  47.7 us
    psum x1, blocking collectives, body(): lax.psum((model_part, loss_part / feat_count), ('rows', 'feat'))  38.9 us
    psum x1, blocking collectives, body(): margin = lax.psum(jnp.sum(partial_value * gap, axis=-1), 'feat')  20.8 us
    psum x1, blocking collectives, body(): square = lax.psum(jnp.sum(grad_proj * grad_proj), 'feat')  12.2 us
    dot_general x1, matrix products, body(): jnp.dot(queries, projection, preferred_element_type=jnp.float32)  11.7 us
    psum x1, waiting for transfers between devices, body(): grad_proj = lax.psum(grad_local, 'rows')  8.61 us
    dot_general x1, matrix products, body(): grad_local = jnp.dot(queries.T, back, preferred_element_type=jnp.float32)  8.29 us
    dot_general x1, matrix products, body(): jnp.dot(pick, coef[:, None] * partial_value, precision=lax.Precision.HIGH...  5.18 us
  transfers between devices with their start and end apart: 1, of which 1 were waited for; matrix products, arithmetic and copies ran while one was open for 3% of the time, Pallas kernels for 0%

commit v1 on v0

--- a/solution.py
+++ b/solution.py
@@ -32,7 +32,7 @@
     pick = pick_table(models, first, second)
     model_part = jnp.dot(pick, coef[:, None] * partial_value, precision=lax.Precision.HIGHEST)
     feat_count = float(lax.axis_size("feat"))
-    grad_models, loss = lax.psum((model_part, loss_part / feat_count), ("rows", "feat"))
+    grad_models, loss = lax.psum(lax.psum((model_part, loss_part / feat_count), "feat"), "rows")
     model_square = jnp.sum(grad_models * grad_models)
     entries = jnp.sqrt(jnp.float32(D * R + NM * R))
     grad_local = jnp.dot(queries.T, back, preferred_element_type=jnp.float32)

time: 178 us -> 210 us (1.18)
  waiting for transfers between devices: 8.62 us -> 47.4 us
  blocking collectives: 71.9 us -> 64.8 us
    psum x1, waiting for transfers between devices: 8.61 us -> 47.4 us  [body(): grad_proj = lax.psum(grad_local, 'rows')]
    psum x1, blocking collectives: 38.9 us -> 23.7 us  [body(): lax.psum(lax.psum((model_part, loss_part / feat_count), 'feat'), 'rows')]
    psum x1, blocking collectives: 12.2 us -> 20.3 us  [body(): square = lax.psum(jnp.sum(grad_proj * grad_proj), 'feat')]
  transfers between devices with their start and end apart: 1 -> 1, of which waited for: 1 -> 1; matrix products, arithmetic and copies ran while one was open for 3% -> 2% of each run, Pallas kernels for 0% -> 0%
where the time goes in v1:
time: 210 us; the launch traced here: 209 us
  blocking collectives  64.8 us (31%)
  local copies, waits for them, and re-layouts  48.7 us (23%)
  waiting for transfers between devices  47.4 us (23%)
  matrix products  25.1 us (12%)
  between operations  16.1 us (8%)
  other arithmetic  6.98 us (3%)
    gather x4, local copies, waits for them, and re-layouts, pair_gap(): return jnp.take(models, first, axis=0) - jnp.take(models, second, axis=0)  47.7 us
    psum x1, waiting for transfers between devices, body(): grad_proj = lax.psum(grad_local, 'rows')  47.4 us
    psum x1, blocking collectives, body(): lax.psum(lax.psum((model_part, loss_part / feat_count), 'feat'), 'rows')  23.7 us
    psum x1, blocking collectives, body(): margin = lax.psum(jnp.sum(partial_value * gap, axis=-1), 'feat')  20.8 us
    psum x1, blocking collectives, body(): square = lax.psum(jnp.sum(grad_proj * grad_proj), 'feat')  20.3 us
    dot_general x1, matrix products, body(): jnp.dot(queries, projection, preferred_element_type=jnp.float32)  11.7 us
    dot_general x1, matrix products, body(): grad_local = jnp.dot(queries.T, back, preferred_element_type=jnp.float32)  8.29 us
    dot_general x1, matrix products, body(): jnp.dot(pick, coef[:, None] * partial_value, precision=lax.Precision.HIGH...  5.18 us
  transfers between devices with their start and end apart: 1, of which 1 were waited for; matrix products, arithmetic and copies ran while one was open for 2% of the time, Pallas kernels for 0%

profile of v1, /device:TPU:0, one launch (start us, length us, event | category | flops | bytes accessed | tf_op | source)
XLA Modules:
  0.0 209.2 jit_solution(1187915647221988299)
XLA Ops:
  7.2 0.0 copy-start
  7.2 0.0 copy-start.1
  7.2 0.0 all-reduce.4.cloned.1.call-start
  7.2 0.7 fusion.14
  8.0 0.8 compare_and_fusion
  8.8 0.7 fusion.13
  9.5 0.0 copy-done.1
  9.5 20.9 %gather_fusion.1 = f32[6144,128]{1,0:T(8,128)} fusion(f32[64,128]{1,0:T(8,128)S(1)} %copy-done.1, s32[6144]{0:T(1024)S(1)} %fusion.14), kind=kCustom, calls=%fused_computation.1.clone | custom fusion | bytes 6316032 | tf_op jit(solution)/shard_map/jit(_take)/gather | solution.py:12
  30.4 2.4 %copy.10 = f32[6144,128]{0,1:T(8,128)S(1)} copy(f32[6144,128]{1,0:T(8,128)} %gather_fusion.1) | data formatting | bytes 6291456 | tf_op jit(solution)/shard_map/jit(_take)/gather | solution.py:12
  32.8 20.9 %gather_fusion = f32[6144,128]{1,0:T(8,128)} fusion(f32[64,128]{1,0:T(8,128)S(1)} %copy-done.1, s32[6144]{0:T(1024)S(1)} %fusion.13), kind=kCustom, calls=%fused_computation.clone | custom fusion | bytes 6316032 | tf_op jit(solution)/shard_map/jit(_take)/gather | solution.py:12
  53.7 3.5 %copy.9 = f32[6144,128]{0,1:T(8,128)} copy(f32[6144,128]{1,0:T(8,128)} %gather_fusion) | data formatting | bytes 6291456 | tf_op jit(solution)/shard_map/jit(_take)/gather | solution.py:12
  57.2 0.0 copy-done
  57.2 0.0 copy-start.4
  57.2 11.7 %multiply_reduce_fusion = (f32[6144]{0:T(1024)S(1)}, f32[6144,128]{0,1:T(8,128)}) fusion(f32[6144,128]{0,1:T(8,128)S(1)} %copy.10, pred[6144]{0:T(1024)(128)(4,1)S(1)} %get-tuple-element.16, f32[6144,128]{0,1:T(8,128)} %copy.9, pred[6144]{0:T(1024)(128)(4,1)S(1)} %get-tuple-element.17, bf16[6144,1024]{1,0:T(8,128)(2,1)} %param.8, ...), kind=kOutput, calls=%fused_computation.6 | convolution fusion | flops 1614538752 | bytes 22319104 | tf_op jit(solution)/shard_map/dot_general | solution.py:25
  68.9 20.8 %psum.49 = f32[6144]{0:T(1024)S(1)} all-reduce(f32[6144]{0:T(1024)S(1)} %get-tuple-element.14), channel_id=1, replica_groups=mesh['rows'=8,'feat'=4] {'feat'}, use_global_device_ids=true, to_apply=%region_1.3 | all-reduce | flops 6144 | bytes 49152 | tf_op jit(solution)/shard_map/psum | solution.py:27
  89.6 0.0 copy-done.4
  89.6 0.6 fusion.11
  90.3 0.0 copy-start.2
  90.3 0.0 copy-start.3
  90.3 8.3 %fusion.8 = f32[1024,128]{0,1:T(8,128)} fusion(bf16[6144,1024]{1,0:T(8,128)(2,1)} %param.8, f32[6144]{0:T(1024)S(1)} %get-tuple-element.13, f32[6144,128]{0,1:T(8,128)S(1)} %copy.10, f32[6144,128]{0,1:T(8,128)} %copy.9, pred[6144]{0:T(1024)(128)(4,1)S(1)} %get-tuple-element.16, pred[6144]{0:T(1024)(128)(4,1)S(1)} %get-tuple-element.17), kind=kOutput, calls=%fused_computation.15 | convolution fusion | flops 1614544896 | bytes 19435520 | tf_op jit(solution)/shard_map/dot_general | solution.py:38
  98.6 0.0 all-reduce.4.cloned.1.call-update
  99.2 0.0 copy-done.2
  99.2 0.0 copy-done.3
  99.3 5.2 %fusion = f32[64,128]{1,0:T(8,128)S(1)} fusion(f32[6144,128]{0,1:T(8,128)} %get-tuple-element.15, f32[6144]{0:T(1024)S(1)} %get-tuple-element.13, s32[6144]{0:T(1024)S(1)} %copy-done.2, s32[6144]{0:T(1024)S(1)} %copy-done.3), kind=kOutput, calls=%fused_computation.3 | convolution fusion | flops 606732288 | bytes 3252224 | tf_op jit(solution)/shard_map/dot_general | solution.py:33
  104.4 47.4 %all-reduce.4.cloned.1.call-done = f32[1024,128]{0,1:T(8,128)} async-done(((f32[1024,128]{0,1:T(8,128)}), f32[1024,128]{0,1:T(8,128)}) %all-reduce.4.cloned.1.call-update) | async-done | bytes 524304 | tf_op jit(solution)/shard_map/psum | solution.py:39
  151.8 1.8 multiply_reduce_fusion.1
  153.6 20.3 %all-reduce.1 = (f32[]{:T(128)}, f32[64,128]{1,0:T(8,128)S(1)}, f32[]{:T(128)}) all-reduce(f32[]{:T(128)} %multiply_reduce_fusion.1, f32[64,128]{1,0:T(8,128)S(1)} %fusion, f32[]{:T(128)S(6)} %div.20), channel_id=1, replica_groups=mesh['rows'=8,'feat'=4] {'feat'}, use_global_device_ids=true, to_apply=%region_4.6 | all-reduce | flops 8194 | bytes 65552 | tf_op jit(solution)/shard_map/psum | solution.py:40
  173.9 23.7 %all-reduce = (f32[64,128]{1,0:T(8,128)S(1)}, f32[]{:T(128)}) all-reduce(f32[64,128]{1,0:T(8,128)S(1)} %get-tuple-element.10, f32[]{:T(128)} %get-tuple-element.11), channel_id=1, replica_groups=mesh['rows'=8,'feat'=4] {'rows'}, use_global_device_ids=true, to_apply=%region_6.8 | all-reduce | flops 8193 | bytes 65544 | tf_op jit(solution)/shard_map/psum | solution.py:35
  197.6 0.6 multiply_reduce_fusion.2
  199.6 0.6 broadcast_multiply_fusion.1
  200.2 1.1 broadcast_multiply_fusion
  201.3 1.0 copy.11
Async XLA Ops:
  7.2 50.0 %copy-start = (bf16[1024,128]{1,0:T(8,128)(2,1)S(1)}, bf16[1024,128]{1,0:T(8,128)(2,1)}, u32[]{:S(2)}) copy-start(bf16[1024,128]{1,0:T(8,128)(2,1)} %param.9) | copy-start | bytes 786436
  7.2 2.3 %copy-start.1 = (f32[64,128]{1,0:T(8,128)S(1)}, f32[64,128]{1,0:T(8,128)}, u32[]{:S(2)}) copy-start(f32[64,128]{1,0:T(8,128)} %param.10) | copy-start | bytes 98308
  7.2 144.6 %all-reduce.4.cloned.1.call-start = ((), (), s32[]{:S(2)}) async-start(), calls=%async_computation | async-start | bytes 1048576 | tf_op jit(solution)/shard_map/psum | solution.py:39
  57.2 32.4 %copy-start.4 = (s32[6144]{0:T(1024)S(1)}, s32[6144]{0:T(1024)}, u32[]{:S(2)}) copy-start(s32[6144]{0:T(1024)} %param.13) | copy-start | bytes 73732
  90.3 9.0 %copy-start.2 = (s32[6144]{0:T(1024)S(1)}, s32[6144]{0:T(1024)}, u32[]{:S(2)}) copy-start(s32[6144]{0:T(1024)} %param.12) | copy-start | bytes 73732
  90.3 9.0 %copy-start.3 = (s32[6144]{0:T(1024)S(1)}, s32[6144]{0:T(1024)}, u32[]{:S(2)}) copy-start(s32[6144]{0:T(1024)} %param.11) | copy-start | bytes 73732
Sparse Core Ops, SparseCore 0:
  98.7 53.0 all-reduce.3

commit v2 on v0

--- a/solution.py
+++ b/solution.py
@@ -24,7 +24,7 @@
     total_rows = float(local_rows * lax.axis_size("rows"))
     partial_value = jnp.dot(queries, projection, preferred_element_type=jnp.float32)
     gap = pair_gap(models, first, second)
-    margin = lax.psum(jnp.sum(partial_value * gap, axis=-1), "feat")
+    margin = jnp.sum(lax.all_gather(jnp.sum(partial_value * gap, axis=-1), "feat"), axis=0)
     sign = 2.0 * wins.astype(jnp.float32) - 1.0
     loss_part = jnp.sum(jax.nn.softplus(-sign * margin)) / total_rows
     coef = -sign * jax.nn.sigmoid(-sign * margin) / total_rows

time: 178 us -> 177 us (level)
  blocking collectives: 71.9 us -> 68.6 us
    psum x1 -> x0, blocking collectives: 20.8 us -> none  [body(): margin = lax.psum(jnp.sum(partial_value * gap, axis=-1), 'feat')]
    all_gather x0 -> x1, blocking collectives: none -> 15.8 us  [body(): lax.all_gather(jnp.sum(partial_value * gap, axis=-1), 'feat')]
where the time goes in v2:
time: 177 us
  blocking collectives  68.6 us (39%)
  local copies, waits for them, and re-layouts  49.6 us (28%)
  matrix products  25.1 us (14%)
  between operations  16.1 us (9%)
  waiting for transfers between devices  9.5 us (5%)
  other arithmetic  7.79 us (4%)
    gather x4, local copies, waits for them, and re-layouts, pair_gap(): return jnp.take(models, first, axis=0) - jnp.take(models, second, axis=0)  47.7 us
    psum x1, blocking collectives, body(): lax.psum((model_part, loss_part / feat_count), ('rows', 'feat'))  40.6 us
    all_gather x1, blocking collectives, body(): lax.all_gather(jnp.sum(partial_value * gap, axis=-1), 'feat')  15.8 us
    psum x1, blocking collectives, body(): square = lax.psum(jnp.sum(grad_proj * grad_proj), 'feat')  12.2 us
    dot_general x1, matrix products, body(): jnp.dot(queries, projection, preferred_element_type=jnp.float32)  11.7 us
    psum x1, waiting for transfers between devices, body(): grad_proj = lax.psum(grad_local, 'rows')  9.48 us
    dot_general x1, matrix products, body(): grad_local = jnp.dot(queries.T, back, preferred_element_type=jnp.float32)  8.3 us
    dot_general x1, matrix products, body(): jnp.dot(pick, coef[:, None] * partial_value, precision=lax.Precision.HIGH...  5.18 us
  transfers between devices with their start and end apart: 1, of which 1 were waited for; matrix products, arithmetic and copies ran while one was open for 3% of the time, Pallas kernels for 0%

profile of v2, /device:TPU:0, one launch (start us, length us, event | category | flops | bytes accessed | tf_op | source)
XLA Modules:
  0.0 176.8 jit_solution(16010385843986132528)
XLA Ops:
  7.2 0.0 copy-start
  7.2 0.0 copy-start.1
  7.2 0.0 all-reduce.3.cloned.1.call-start
  7.2 0.7 fusion.13
  8.0 0.8 compare_and_fusion
  8.8 0.7 fusion.14
  9.5 0.0 copy-done.1
  9.5 20.9 %gather_fusion = f32[6144,128]{1,0:T(8,128)} fusion(f32[64,128]{1,0:T(8,128)S(1)} %copy-done.1, s32[6144]{0:T(1024)S(1)} %fusion.13), kind=kCustom, calls=%fused_computation.clone | custom fusion | bytes 6316032 | tf_op jit(solution)/shard_map/jit(_take)/gather | solution.py:12
  30.4 2.4 %copy.15 = f32[6144,128]{0,1:T(8,128)S(1)} copy(f32[6144,128]{1,0:T(8,128)} %gather_fusion) | data formatting | bytes 6291456 | tf_op jit(solution)/shard_map/jit(_take)/gather | solution.py:12
  32.8 20.9 %gather_fusion.1 = f32[6144,128]{1,0:T(8,128)} fusion(f32[64,128]{1,0:T(8,128)S(1)} %copy-done.1, s32[6144]{0:T(1024)S(1)} %fusion.14), kind=kCustom, calls=%fused_computation.1.clone | custom fusion | bytes 6316032 | tf_op jit(solution)/shard_map/jit(_take)/gather | solution.py:12
  53.7 3.5 %copy.16 = f32[6144,128]{0,1:T(8,128)} copy(f32[6144,128]{1,0:T(8,128)} %gather_fusion.1) | data formatting | bytes 6291456 | tf_op jit(solution)/shard_map/jit(_take)/gather | solution.py:12
  57.2 0.0 copy-done
  57.2 11.7 %multiply_reduce_fusion = (f32[6144]{0:T(1024)S(1)}, f32[6144,128]{0,1:T(8,128)}) fusion(f32[6144,128]{0,1:T(8,128)} %copy.16, pred[6144]{0:T(1024)(128)(4,1)S(1)} %get-tuple-element.19, f32[6144,128]{0,1:T(8,128)S(1)} %copy.15, pred[6144]{0:T(1024)(128)(4,1)S(1)} %get-tuple-element.20, bf16[6144,1024]{1,0:T(8,128)(2,1)} %param.8, ...), kind=kOutput, calls=%fused_computation.6 | convolution fusion | flops 1614538752 | bytes 22319104 | tf_op jit(solution)/shard_map/dot_general | solution.py:25
  68.9 15.8 %all-gather = f32[24576]{0:T(1024)} all-gather(f32[6144]{0:T(1024)S(1)} %get-tuple-element.17), channel_id=2, replica_groups=mesh['rows'=8,'feat'=4] {'feat'}, dimensions={0}, use_global_device_ids=true | all-gather | bytes 122880 | tf_op jit(solution)/shard_map/all_gather | solution.py:27
  84.6 0.9 reshape.30
  85.6 0.1 reduce_sum.46
  85.6 1.4 fusion.11
  87.0 0.0 copy-start.2
  87.0 0.0 copy-start.3
  87.0 8.3 %fusion.8 = f32[1024,128]{0,1:T(8,128)} fusion(bf16[6144,1024]{1,0:T(8,128)(2,1)} %param.8, f32[6144]{0:T(1024)S(1)} %get-tuple-element.16, f32[6144,128]{0,1:T(8,128)} %copy.16, f32[6144,128]{0,1:T(8,128)S(1)} %copy.15, pred[6144]{0:T(1024)(128)(4,1)S(1)} %get-tuple-element.19, pred[6144]{0:T(1024)(128)(4,1)S(1)} %get-tuple-element.20), kind=kOutput, calls=%fused_computation.15 | convolution fusion | flops 1614544896 | bytes 19435520 | tf_op jit(solution)/shard_map/dot_general | solution.py:38
  95.3 0.0 all-reduce.3.cloned.1.call-update
  96.0 0.0 copy-done.2
  96.0 0.0 copy-done.3
  96.0 5.2 %fusion = f32[64,128]{1,0:T(8,128)S(1)} fusion(f32[6144,128]{0,1:T(8,128)} %get-tuple-element.18, f32[6144]{0:T(1024)S(1)} %get-tuple-element.16, s32[6144]{0:T(1024)S(1)} %copy-done.2, s32[6144]{0:T(1024)S(1)} %copy-done.3), kind=kOutput, calls=%fused_computation.3 | convolution fusion | flops 606732288 | bytes 3252224 | tf_op jit(solution)/shard_map/dot_general | solution.py:33
  101.2 40.6 %all-reduce = (f32[64,128]{1,0:T(8,128)S(1)}, f32[]{:T(128)}) all-reduce(f32[64,128]{1,0:T(8,128)S(1)} %fusion, f32[]{:T(128)S(6)} %div.20), channel_id=1, replica_groups=mesh['rows'=8,'feat'=4] {'rows','feat'}, use_global_device_ids=true, to_apply=%region_5.7 | all-reduce | flops 8193 | bytes 65544 | tf_op jit(solution)/shard_map/psum | solution.py:35
  141.8 9.5 %all-reduce.3.cloned.1.call-done = f32[1024,128]{0,1:T(8,128)} async-done(((f32[1024,128]{0,1:T(8,128)}), f32[1024,128]{0,1:T(8,128)}) %all-reduce.3.cloned.1.call-update) | async-done | bytes 524304 | tf_op jit(solution)/shard_map/psum | solution.py:39
  151.3 1.8 %multiply_reduce_fusion.1 = f32[]{:T(128)} fusion(f32[1024,128]{0,1:T(8,128)} %all-reduce.3.cloned.1.call-done), kind=kLoop, calls=%fused_computation.18 | loop fusion | flops 262143 | bytes 524292 | tf_op jit(solution)/shard_map/reduce_sum | solution.py:40
  153.1 0.6 multiply_reduce_fusion.2
  153.7 12.2 %psum.29 = f32[]{:T(128)} all-reduce(f32[]{:T(128)} %multiply_reduce_fusion.1), channel_id=1, replica_groups=mesh['rows'=8,'feat'=4] {'feat'}, use_global_device_ids=true, to_apply=%region_4.6 | all-reduce | flops 1 | bytes 8 | tf_op jit(solution)/shard_map/psum | solution.py:40
  167.3 0.6 broadcast_multiply_fusion.1
  167.9 1.1 broadcast_multiply_fusion
  169.0 1.0 copy.17
Async XLA Ops:
  7.2 50.0 %copy-start = (bf16[1024,128]{1,0:T(8,128)(2,1)S(1)}, bf16[1024,128]{1,0:T(8,128)(2,1)}, u32[]{:S(2)}) copy-start(bf16[1024,128]{1,0:T(8,128)(2,1)} %param.9) | copy-start | bytes 786436
  7.2 2.3 %copy-start.1 = (f32[64,128]{1,0:T(8,128)S(1)}, f32[64,128]{1,0:T(8,128)}, u32[]{:S(2)}) copy-start(f32[64,128]{1,0:T(8,128)} %param.10) | copy-start | bytes 98308
  7.2 144.1 %all-reduce.3.cloned.1.call-start = ((), (), s32[]{:S(2)}) async-start(), calls=%async_computation | async-start | bytes 1048576 | tf_op jit(solution)/shard_map/psum | solution.py:39
  87.0 9.0 %copy-start.2 = (s32[6144]{0:T(1024)S(1)}, s32[6144]{0:T(1024)}, u32[]{:S(2)}) copy-start(s32[6144]{0:T(1024)} %param.12) | copy-start | bytes 73732
  87.0 9.0 %copy-start.3 = (s32[6144]{0:T(1024)S(1)}, s32[6144]{0:T(1024)}, u32[]{:S(2)}) copy-start(s32[6144]{0:T(1024)} %param.11) | copy-start | bytes 73732
Sparse Core Ops, SparseCore 0:
  95.5 55.7 all-reduce.2
